TPU v7x, 512 devices: a whole 4x8x8 slice. The times are simulated.
512 devices in a mesh: chan: 8 (over z), sx: 8 (over x, core), sy: 8 (over y).
Axes of the slice: x: 4, y: 8, z: 8, core: 2. Of those that a mesh axis runs over, the one named last changes fastest.
Arguments:
- volume: bfloat16 [8, 64, 64, 256], P('sx', 'sy', None, 'chan'), may hold values from -6 to 6
- kernel: bfloat16 [27, 256, 256], P(None, 'chan'), may hold values from -0.078125 to 0.078125
- grad_out: bfloat16 [8, 64, 64, 256], P('sx', 'sy', None, 'chan'), may hold values from -6 to 6
Outputs:
- out: bfloat16 [8, 64, 64, 256], P('sx', 'sy', None, 'chan')
- grad_input: bfloat16 [8, 64, 64, 256], P('sx', 'sy', None, 'chan')
- grad_kernel: float32 [27, 256, 256], P(None, 'chan')
All inputs are finite; a program needn't handle non-finite values.
Results may differ from a plain program's by a relative error of at most 0.0015.
Values may be sent and summed in bfloat16 or wider, within the bound.
No kernel may reach another device: no remote copies, remote signals or barrier semaphores. Data moves between devices by JAX's collectives and lax.ppermute only.
A program may use at most 64 MiB of HBM per device.

v0:
```python
import math
import jax
import jax.numpy as jnp
from jax import lax
from jax.sharding import PartitionSpec as P


def padded_2(shard, sides, width):
    for axis, dim in sides:
        count, length = (lax.axis_size(axis), shard.shape[dim])
        up = [(i, (i + 1) % count) for i in range(count - 1)]
        down = [(j, i) for i, j in up]
        last = lax.slice_in_dim(shard, length - width, length, axis=dim)
        leading = lax.slice_in_dim(shard, 0, width, axis=dim)
        before = lax.ppermute(last, axis, up)
        after = lax.ppermute(leading, axis, down)
        shard = jnp.concatenate([before, shard, after], axis=dim)
    return shard


def body(volume, kernel, grad_out):
    size_x, size_y, size_z, own_in = volume.shape
    total_out = kernel.shape[2]
    cells = size_x * size_y * size_z
    rim = padded_2(volume, (("sx", 0), ("sy", 1)), 1)
    padded = jnp.pad(rim, ((0, 0), (0, 0), (1, 1), (0, 0)))
    offsets = [(index // 9, index // 3 % 3, index % 3) for index in range(27)]
    partial_out = jnp.zeros((cells, total_out), jnp.float32)
    for index in range(27):
        a, b, e = offsets[index]
        window = padded[a : a + size_x, b : b + size_y, e : e + size_z].reshape(cells, own_in)
        partial_out = partial_out + jnp.dot(
            window, kernel[index], preferred_element_type=jnp.float32
        )
    partial_out = partial_out.reshape(size_x, size_y, size_z, total_out)
    out = lax.psum_scatter(partial_out, "chan", scatter_dimension=3, tiled=True).astype(
        jnp.bfloat16
    )
    grad_full = lax.all_gather(grad_out, "chan", axis=3, tiled=True)
    grad_rimmed = padded_2(grad_full, (("sx", 0), ("sy", 1)), 1)
    grad_padded = jnp.pad(grad_rimmed, ((0, 0), (0, 0), (1, 1), (0, 0)))
    flat_grad = grad_full.reshape(cells, total_out)
    back = jnp.zeros((cells, own_in), jnp.float32)
    kernel_terms = []
    for index in range(27):
        a, b, e = offsets[index]
        window = grad_padded[
            2 - a : 2 - a + size_x, 2 - b : 2 - b + size_y, 2 - e : 2 - e + size_z
        ].reshape(cells, total_out)
        back = back + lax.dot_general(
            window, kernel[index], (((1,), (1,)), ((), ())), preferred_element_type=jnp.float32
        )
        in_window = padded[a : a + size_x, b : b + size_y, e : e + size_z].reshape(cells, own_in)
        kernel_terms.append(
            lax.dot_general(
                in_window, flat_grad, (((0,), (0,)), ((), ())), preferred_element_type=jnp.float32
            )
        )
    grad_input = back.reshape(size_x, size_y, size_z, own_in).astype(jnp.bfloat16)
    local_kernel = jnp.stack(kernel_terms)
    summed = lax.psum(local_kernel, ("sx", "sy"))
    all_cells = cells * lax.axis_size("sx") * lax.axis_size("sy")
    grad_kernel = summed / jnp.float32(math.sqrt(all_cells))
    return (out, grad_input, grad_kernel)


def solution(mesh):
    return jax.shard_map(
        body,
        mesh=mesh,
        in_specs=(P("sx", "sy", None, "chan"), P(None, "chan", None), P("sx", "sy", None, "chan")),
        out_specs=(P("sx", "sy", None, "chan"), P("sx", "sy", None, "chan"), P(None, "chan", None)),
        check_vma=False,
    )
```

profile of v0, /device:TPU:25, one launch (start us, length us, event | category | flops | bytes accessed | tf_op | source)
XLA Modules:
  0.0 342.9 jit_solution(3898932481704692713)
XLA Ops:
  8.1 3.7 %collective-permute-start = (bf16[1,8,64,32]{2,3,1,0:T(8,128)(2,1)}, bf16[1,8,64,32]{2,3,1,0:T(8,128)(2,1)S(1)}, u32[]{:S(2)}, u32[]{:S(2)}) collective-permute-start(bf16[1,8,64,32]{2,3,1,0:T(8,128)(2,1)} %param.3), channel_id=1, source_target_pairs={{0,8},{8,16},{16,24},{24,32},{32,40},{40,48},{48,56},{1,9},{9,17},... | collective-permute-start | bytes 98312 | tf_op jit(solution)/shard_map/ppermute | solution.py:15
  11.7 1.9 collective-permute-start.1
  15.5 2.1 collective-permute-done.1
  17.6 2.1 collective-permute-start.3
  19.7 4.4 %collective-permute-start.2 = (bf16[3,1,64,32]{2,3,1,0:T(8,128)(2,1)S(1)}, bf16[3,1,64,32]{2,3,1,0:T(8,128)(2,1)S(1)}, u32[]{:S(2)}, u32[]{:S(2)}) collective-permute-start(bf16[3,1,64,32]{2,3,1,0:T(8,128)(2,1)S(1)} %get-tuple-element.68), channel_id=1, source_target_pairs={{0,1},{1,2},{2,3},{3,4},{4,5},{5,6},{6,7},{8,9},{9,10},{10,11},{11... | collective-permute-start | bytes 36872 | tf_op jit(solution)/shard_map/ppermute | solution.py:15
  24.1 26.2 %all_gather.3 = bf16[1,8,64,256]{2,1,0,3:T(8,128)(2,1)S(1)} all-gather(bf16[1,8,64,32]{2,1,0,3:T(8,128)(2,1)S(1)} %copy.98), channel_id=1, replica_groups=mesh['chan'=8,'sx'=8,'sy'=8] {'chan'}, dimensions={3}, use_global_device_ids=true | all-gather | bytes 294912 | tf_op jit(solution)/shard_map/all_gather | solution.py:39
  50.6 5.5 %collective-permute-start.5 = (bf16[1,8,64,256]{3,2,1,0:T(8,128)(2,1)S(1)}, bf16[1,8,64,256]{3,2,1,0:T(8,128)(2,1)S(1)}, u32[]{:S(2)}, u32[]{:S(2)}) collective-permute-start(bf16[1,8,64,256]{3,2,1,0:T(8,128)(2,1)S(1)} %copy.99), channel_id=1, source_target_pairs={{8,0},{16,8},{24,16},{32,24},{40,32},{48,40},{56,48},{9,1},{17,9},... | collective-permute-start | bytes 786440 | tf_op jit(solution)/shard_map/ppermute | solution.py:16
  56.1 4.7 %collective-permute-start.4 = (bf16[1,8,64,256]{3,2,1,0:T(8,128)(2,1)S(1)}, bf16[1,8,64,256]{3,2,1,0:T(8,128)(2,1)S(1)}, u32[]{:S(2)}, u32[]{:S(2)}) collective-permute-start(bf16[1,8,64,256]{3,2,1,0:T(8,128)(2,1)S(1)} %copy.99), channel_id=1, source_target_pairs={{0,8},{8,16},{16,24},{24,32},{32,40},{40,48},{48,56},{1,9},{9,17},... | collective-permute-start | bytes 786440 | tf_op jit(solution)/shard_map/ppermute | solution.py:15
  74.5 1.6 reshape.329
  77.6 1.6 reshape.330
  79.2 1.5 copy.78
  80.6 1.6 reshape.331
  83.7 1.6 reshape.332
  85.9 1.6 reshape.333
  88.1 1.6 reshape.334
  90.3 1.6 reshape.335
  93.4 1.6 reshape.337
  96.4 1.6 reshape.338
  98.7 1.6 reshape.339
  100.9 1.6 reshape.340
  102.4 1.5 copy.88
  103.9 1.6 reshape.341
  106.1 1.6 reshape.342
  107.7 1.5 copy.90
  109.2 1.6 reshape.343
  112.2 1.6 reshape.344
  114.5 1.6 reshape.347
  146.8 1.9 collective-permute-start.7
  148.7 4.8 %collective-permute-start.6 = (bf16[3,1,64,256]{3,2,1,0:T(8,128)(2,1)S(1)}, bf16[3,1,64,256]{3,2,1,0:T(8,128)(2,1)S(1)}, u32[]{:S(2)}, u32[]{:S(2)}) collective-permute-start(bf16[3,1,64,256]{3,2,1,0:T(8,128)(2,1)S(1)} %get-tuple-element.39), channel_id=1, source_target_pairs={{0,1},{1,2},{2,3},{3,4},{4,5},{5,6},{6,7},{8,9},{9,10},{10,11},{11... | collective-permute-start | bytes 294920 | tf_op jit(solution)/shard_map/ppermute | solution.py:15
  162.8 168.9 %all-reduce.4.cloned.1.call-done = f32[27,32,256]{2,1,0:T(8,128)} async-done(((f32[27,32,256]{2,1,0:T(8,128)}), f32[27,32,256]{2,1,0:T(8,128)}) %all-reduce.4.cloned.1.call-update) | async-done | bytes 884752 | tf_op jit(solution)/shard_map/psum | solution.py:61
  331.7 2.2 broadcast_multiply_fusion
  333.9 1.5 convert_element_type.21
  (221 shorter events, 67.4 us)
Async XLA Ops:
  8.0 52.8 %copy-start.4 = (bf16[1,8,64,32]{2,3,1,0:T(8,128)(2,1)S(1)}, bf16[1,8,64,32]{2,3,1,0:T(8,128)(2,1)}, u32[]{:S(2)}) copy-start(bf16[1,8,64,32]{2,3,1,0:T(8,128)(2,1)} %param.3) | copy-start | bytes 98308
  8.0 323.7 %all-reduce.4.cloned.1.call-start = ((), (), s32[]{:S(2)}) async-start(), calls=%async_computation.2 | async-start | bytes 1769472 | tf_op jit(solution)/shard_map/psum | solution.py:61
  8.1 6.5 %collective-permute-start = (bf16[1,8,64,32]{2,3,1,0:T(8,128)(2,1)}, bf16[1,8,64,32]{2,3,1,0:T(8,128)(2,1)S(1)}, u32[]{:S(2)}, u32[]{:S(2)}) collective-permute-start(bf16[1,8,64,32]{2,3,1,0:T(8,128)(2,1)} %param.3), channel_id=1, source_target_pairs={{0,8},{8,16},{16,24},{24,32},{32,40},{40,48},{48,56},{1,9},{9,17},... | collective-permute-start | bytes 98312 | tf_op jit(solution)/shard_map/ppermute | solution.py:15
  11.7 5.8 %collective-permute-start.1 = (bf16[1,8,64,32]{2,3,1,0:T(8,128)(2,1)}, bf16[1,8,64,32]{2,3,1,0:T(8,128)(2,1)S(1)}, u32[]{:S(2)}, u32[]{:S(2)}) collective-permute-start(bf16[1,8,64,32]{2,3,1,0:T(8,128)(2,1)} %param.3), channel_id=1, source_target_pairs={{8,0},{16,8},{24,16},{32,24},{40,32},{48,40},{56,48},{9,1},{17,9},... | collective-permute-start | bytes 98312 | tf_op jit(solution)/shard_map/ppermute | solution.py:16
  14.6 47.1 %copy-start.8 = (bf16[1,8,64,32]{2,3,1,0:T(8,128)(2,1)}, bf16[1,8,64,32]{2,3,1,0:T(8,128)(2,1)S(1)}, u32[]{:S(2)}) copy-start(bf16[1,8,64,32]{2,3,1,0:T(8,128)(2,1)S(1)} %collective-permute-done) | copy-start | bytes 98308
  17.5 45.0 %copy-start.6 = (bf16[1,8,64,32]{2,3,1,0:T(8,128)(2,1)}, bf16[1,8,64,32]{2,3,1,0:T(8,128)(2,1)S(1)}, u32[]{:S(2)}) copy-start(bf16[1,8,64,32]{2,3,1,0:T(8,128)(2,1)S(1)} %collective-permute-done.1) | copy-start | bytes 98308
  17.6 44.9 %collective-permute-start.3 = (bf16[3,1,64,32]{2,3,1,0:T(8,128)(2,1)S(1)}, bf16[3,1,64,32]{2,3,1,0:T(8,128)(2,1)S(1)}, u32[]{:S(2)}, u32[]{:S(2)}) collective-permute-start(bf16[3,1,64,32]{2,3,1,0:T(8,128)(2,1)S(1)} %get-tuple-element.69), channel_id=1, source_target_pairs={{1,0},{2,1},{3,2},{4,3},{5,4},{6,5},{7,6},{9,8},{10,9},{11,10},{12... | collective-permute-start | bytes 36872 | tf_op jit(solution)/shard_map/ppermute | solution.py:16
  19.7 42.9 %collective-permute-start.2 = (bf16[3,1,64,32]{2,3,1,0:T(8,128)(2,1)S(1)}, bf16[3,1,64,32]{2,3,1,0:T(8,128)(2,1)S(1)}, u32[]{:S(2)}, u32[]{:S(2)}) collective-permute-start(bf16[3,1,64,32]{2,3,1,0:T(8,128)(2,1)S(1)} %get-tuple-element.68), channel_id=1, source_target_pairs={{0,1},{1,2},{2,3},{3,4},{4,5},{5,6},{6,7},{8,9},{9,10},{10,11},{11... | collective-permute-start | bytes 36872 | tf_op jit(solution)/shard_map/ppermute | solution.py:15
  50.6 96.1 %collective-permute-start.5 = (bf16[1,8,64,256]{3,2,1,0:T(8,128)(2,1)S(1)}, bf16[1,8,64,256]{3,2,1,0:T(8,128)(2,1)S(1)}, u32[]{:S(2)}, u32[]{:S(2)}) collective-permute-start(bf16[1,8,64,256]{3,2,1,0:T(8,128)(2,1)S(1)} %copy.99), channel_id=1, source_target_pairs={{8,0},{16,8},{24,16},{32,24},{40,32},{48,40},{56,48},{9,1},{17,9},... | collective-permute-start | bytes 786440 | tf_op jit(solution)/shard_map/ppermute | solution.py:16
  56.1 90.7 %collective-permute-start.4 = (bf16[1,8,64,256]{3,2,1,0:T(8,128)(2,1)S(1)}, bf16[1,8,64,256]{3,2,1,0:T(8,128)(2,1)S(1)}, u32[]{:S(2)}, u32[]{:S(2)}) collective-permute-start(bf16[1,8,64,256]{3,2,1,0:T(8,128)(2,1)S(1)} %copy.99), channel_id=1, source_target_pairs={{0,8},{8,16},{16,24},{24,32},{32,40},{40,48},{48,56},{1,9},{9,17},... | collective-permute-start | bytes 786440 | tf_op jit(solution)/shard_map/ppermute | solution.py:15
  63.9 2.3 copy-start
  68.5 18.9 %copy-start.14 = (bf16[1,8,64,32]{2,3,1,0:T(8,128)(2,1)S(1)}, bf16[1,8,64,32]{2,3,1,0:T(8,128)(2,1)}, u32[]{:S(2)}) copy-start(bf16[1,8,64,32]{2,3,1,0:T(8,128)(2,1)} %get-tuple-element.51) | copy-start | bytes 98308
  68.5 21.2 %copy-start.13 = (bf16[1,8,64,32]{2,3,1,0:T(8,128)(2,1)S(1)}, bf16[1,8,64,32]{2,3,1,0:T(8,128)(2,1)}, u32[]{:S(2)}) copy-start(bf16[1,8,64,32]{2,3,1,0:T(8,128)(2,1)} %get-tuple-element.50) | copy-start | bytes 98308
  74.5 25.7 %copy-start.12 = (bf16[1,8,64,32]{2,3,1,0:T(8,128)(2,1)S(1)}, bf16[1,8,64,32]{2,3,1,0:T(8,128)(2,1)}, u32[]{:S(2)}) copy-start(bf16[1,8,64,32]{2,3,1,0:T(8,128)(2,1)} %get-tuple-element.47) | copy-start | bytes 98308
  88.1 25.7 %copy-start.11 = (bf16[1,8,64,32]{2,3,1,0:T(8,128)(2,1)S(1)}, bf16[1,8,64,32]{2,3,1,0:T(8,128)(2,1)}, u32[]{:S(2)}) copy-start(bf16[1,8,64,32]{2,3,1,0:T(8,128)(2,1)} %get-tuple-element.42) | copy-start | bytes 98308
  90.3 25.7 %copy-start.3 = (bf16[1,8,64,32]{2,3,1,0:T(8,128)(2,1)S(1)}, bf16[1,8,64,32]{2,3,1,0:T(8,128)(2,1)}, u32[]{:S(2)}) copy-start(bf16[1,8,64,32]{2,3,1,0:T(8,128)(2,1)} %copy-done.2) | copy-start | bytes 98308
  102.4 16.1 %copy-start.9 = (bf16[1,8,64,32]{2,3,1,0:T(8,128)(2,1)S(1)}, bf16[1,8,64,32]{2,3,1,0:T(8,128)(2,1)}, u32[]{:S(2)}) copy-start(bf16[1,8,64,32]{2,3,1,0:T(8,128)(2,1)} %copy-done.8) | copy-start | bytes 98308
  116.0 5.0 %copy-start.1 = (bf16[1,8,64,32]{2,3,1,0:T(8,128)(2,1)S(1)}, bf16[1,8,64,32]{2,3,1,0:T(8,128)(2,1)}, u32[]{:S(2)}) copy-start(bf16[1,8,64,32]{2,3,1,0:T(8,128)(2,1)} %get-tuple-element.60) | copy-start | bytes 98308
  121.0 5.0 %copy-start.5 = (bf16[1,8,64,32]{2,3,1,0:T(8,128)(2,1)S(1)}, bf16[1,8,64,32]{2,3,1,0:T(8,128)(2,1)}, u32[]{:S(2)}) copy-start(bf16[1,8,64,32]{2,3,1,0:T(8,128)(2,1)} %param.3) | copy-start | bytes 98308
  128.6 5.0 %copy-start.7 = (bf16[1,8,64,32]{2,3,1,0:T(8,128)(2,1)S(1)}, bf16[1,8,64,32]{2,3,1,0:T(8,128)(2,1)}, u32[]{:S(2)}) copy-start(bf16[1,8,64,32]{2,3,1,0:T(8,128)(2,1)} %copy-done.6) | copy-start | bytes 98308
  134.4 3.5 %copy-start.17 = (bf16[512,32]{0,1:T(8,128)(2,1)S(1)}, bf16[512,32]{0,1:T(8,128)(2,1)}, u32[]{:S(2)}) copy-start(bf16[512,32]{0,1:T(8,128)(2,1)} %reshape.324) | copy-start | bytes 98308
  136.9 1.2 copy-start.21
  137.8 196.1 %reduce-scatter.2.cloned.1.call-start = ((), (), s32[]{:S(2)}) async-start(), calls=%async_computation.1 | async-start | bytes 1179648 | tf_op jit(solution)/shard_map/reduce_scatter | solution.py:36
  138.2 0.8 copy-start.16
  138.6 0.8 copy-start.18
  138.9 0.8 copy-start.19
  139.7 0.8 copy-start.22
  140.1 0.8 copy-start.23
  140.4 0.8 copy-start.26
  145.8 0.8 copy-start.10
  146.8 8.3 %collective-permute-start.7 = (bf16[3,1,64,256]{3,2,1,0:T(8,128)(2,1)S(1)}, bf16[3,1,64,256]{3,2,1,0:T(8,128)(2,1)S(1)}, u32[]{:S(2)}, u32[]{:S(2)}) collective-permute-start(bf16[3,1,64,256]{3,2,1,0:T(8,128)(2,1)S(1)} %get-tuple-element.40), channel_id=1, source_target_pairs={{1,0},{2,1},{3,2},{4,3},{5,4},{6,5},{7,6},{9,8},{10,9},{11,10},{12... | collective-permute-start | bytes 294920 | tf_op jit(solution)/shard_map/ppermute | solution.py:16
  148.7 6.4 %collective-permute-start.6 = (bf16[3,1,64,256]{3,2,1,0:T(8,128)(2,1)S(1)}, bf16[3,1,64,256]{3,2,1,0:T(8,128)(2,1)S(1)}, u32[]{:S(2)}, u32[]{:S(2)}) collective-permute-start(bf16[3,1,64,256]{3,2,1,0:T(8,128)(2,1)S(1)} %get-tuple-element.39), channel_id=1, source_target_pairs={{0,1},{1,2},{2,3},{3,4},{4,5},{5,6},{6,7},{8,9},{9,10},{10,11},{11... | collective-permute-start | bytes 294920 | tf_op jit(solution)/shard_map/ppermute | solution.py:15
  (16 other events, 11.7 us)
Sparse Core Ops, SparseCore 0:
  137.9 193.7 all-reduce.3
Sparse Core Ops, SparseCore 1:
  155.2 32.7 reduce-scatter.1
where the time goes:
time: 345 us; the launch traced here: 343 us
  waiting for transfers between devices  171 us (50%)
  local copies, waits for them, and re-layouts  60 us (17%)
  matrix products  34.2 us (10%)
  starting transfers between devices  29 us (8%)
  blocking collectives  26.2 us (8%)
  between operations  16.2 us (5%)
  other arithmetic  6.23 us (2%)
    psum x1, waiting for transfers between devices, body(): summed = lax.psum(local_kernel, ('sx', 'sy'))  169 us
    reshape x27, local copies, waits for them, and re-layouts, body(): padded[a:a + size_x, b:b + size_y, e:e + size_z].reshape(cells, own_in)  29.3 us
    all_gather x1, blocking collectives, body(): grad_full = lax.all_gather(grad_out, 'chan', axis=3, tiled=True)  26.2 us
    dot_general x27, matrix products, body(): lax.dot_general(in_window, flat_grad, (((0,), (0,)), ((), ())), preferred...  22.6 us
    slice x25, local copies, waits for them, and re-layouts, body(): padded[a:a + size_x, b:b + size_y, e:e + size_z].reshape(cells, own_in)  21 us
    ppermute x4, starting transfers between devices, padded_2(): before = lax.ppermute(last, axis, up)  17.6 us
    ppermute x4, starting transfers between devices, padded_2(): after = lax.ppermute(leading, axis, down)  11.4 us
    unnamed x81, local copies, waits for them, and re-layouts  6.98 us
  transfers between devices with their start and end apart: 10, of which 2 were waited for; matrix products, arithmetic and copies ran while one was open for 28% of the time, Pallas kernels for 0%

commit v1 on v0

--- a/solution.py
+++ b/solution.py
@@ -36,7 +36,31 @@
     out = lax.psum_scatter(partial_out, "chan", scatter_dimension=3, tiled=True).astype(
         jnp.bfloat16
     )
-    grad_full = lax.all_gather(grad_out, "chan", axis=3, tiled=True)
+    oldest, top, current_arr = (lax.psum(1, "chan"), lax.axis_index("chan"), grad_out.shape[3])
+    wide_out = v1 = grad_out
+    grad_full = lax.dynamic_update_slice_in_dim(
+        jnp.zeros(
+            [h * oldest if dev_i == 3 else h for dev_i, h in enumerate(grad_out.shape)],
+            grad_out.dtype,
+        ),
+        grad_out,
+        top * current_arr,
+        axis=3,
+    )
+    for tick in range(1, oldest // 2 + 1):
+        wide_out = lax.ppermute(
+            wide_out, "chan", [(dev_i, (dev_i + 1) % oldest) for dev_i in range(oldest)]
+        )
+        grad_full = lax.dynamic_update_slice_in_dim(
+            grad_full, wide_out, (top - tick) % oldest * current_arr, axis=3
+        )
+        if 2 * tick < oldest:
+            v1 = lax.ppermute(
+                v1, "chan", [(dev_i, (dev_i - 1) % oldest) for dev_i in range(oldest)]
+            )
+            grad_full = lax.dynamic_update_slice_in_dim(
+                grad_full, v1, (top + tick) % oldest * current_arr, axis=3
+            )
     grad_rimmed = padded_2(grad_full, (("sx", 0), ("sy", 1)), 1)
     grad_padded = jnp.pad(grad_rimmed, ((0, 0), (0, 0), (1, 1), (0, 0)))
     flat_grad = grad_full.reshape(cells, total_out)

time: 345 us -> 308 us (0.89)
  local copies, waits for them, and re-layouts: 60 us -> 33.3 us
  blocking collectives: 26.2 us -> 0 us
  starting transfers between devices: 29 us -> 53.5 us
  matrix products: 34.2 us -> 17.5 us
  waiting for transfers between devices: 171 us -> 179 us
    ppermute x0 -> x7, starting transfers between devices: none -> 27.7 us  [the longest x3 17.7 us: body(): lax.ppermute(v1, 'chan', [(dev_i, (dev_i - 1) % oldest) for dev_i in rang...]
    all_gather x1 -> x0, blocking collectives: 26.2 us -> none  [body(): grad_full = lax.all_gather(grad_out, 'chan', axis=3, tiled=True)]
    reshape x27, local copies, waits for them, and re-layouts: 29.3 us -> 6.79 us  [body(): padded[a:a + size_x, b:b + size_y, e:e + size_z].reshape(cells, own_in)]
    slice x25, local copies, waits for them, and re-layouts: 21 us -> 2.45 us  [body(): padded[a:a + size_x, b:b + size_y, e:e + size_z].reshape(cells, own_in)]
    dot_general x27, matrix products: 22.6 us -> 5.84 us  [body(): lax.dot_general(in_window, flat_grad, (((0,), (0,)), ((), ())), preferred...]
    dynamic_update_slice x0 -> x8, local copies, waits for them, and re-layouts: none -> 11.8 us  [the longest x4 5.72 us: body(): lax.dynamic_update_slice_in_dim(grad_full, wide_out, (top - tick) % oldes...]
    psum x1, waiting for transfers between devices: 169 us -> 179 us  [body(): summed = lax.psum(local_kernel, ('sx', 'sy'))]
    ppermute x0 -> x7, local copies, waits for them, and re-layouts: none -> 4.2 us  [the longest x4 2.16 us: body(): lax.ppermute(wide_out, 'chan', [(dev_i, (dev_i + 1) % oldest) for dev_i i...]
  transfers between devices with their start and end apart: 10 -> 17, of which waited for: 2 -> 2; matrix products, arithmetic and copies ran while one was open for 28% -> 17% of each run, Pallas kernels for 0% -> 0%
where the time goes in v1:
time: 308 us; the launch traced here: 307 us
  waiting for transfers between devices  179 us (58%)
  starting transfers between devices  53.5 us (17%)
  local copies, waits for them, and re-layouts  33.3 us (11%)
  matrix products  17.5 us (6%)
  between operations  16.8 us (5%)
  other arithmetic  6.35 us (2%)
    psum x1, waiting for transfers between devices, body(): summed = lax.psum(local_kernel, ('sx', 'sy'))  179 us
    ppermute x3, starting transfers between devices, body(): lax.ppermute(v1, 'chan', [(dev_i, (dev_i - 1) % oldest) for dev_i in rang...  17.7 us
    ppermute x4, starting transfers between devices, padded_2(): before = lax.ppermute(last, axis, up)  17.5 us
    ppermute x4, starting transfers between devices, body(): lax.ppermute(wide_out, 'chan', [(dev_i, (dev_i + 1) % oldest) for dev_i i...  9.93 us
    ppermute x4, starting transfers between devices, padded_2(): after = lax.ppermute(leading, axis, down)  8.23 us
    reshape x27, local copies, waits for them, and re-layouts, body(): padded[a:a + size_x, b:b + size_y, e:e + size_z].reshape(cells, own_in)  6.79 us
    dot_general x27, matrix products, body(): jnp.dot(window, kernel[index], preferred_element_type=jnp.float32)  6.63 us
  transfers between devices with their start and end apart: 17, of which 2 were waited for; matrix products, arithmetic and copies ran while one was open for 17% of the time, Pallas kernels for 0%

profile of v1, /device:TPU:25, one launch (start us, length us, event | category | flops | bytes accessed | tf_op | source)
XLA Modules:
  0.0 306.9 jit_solution(12535437286542561735)
XLA Ops:
  8.0 3.7 %collective-permute-start = (bf16[1,8,64,32]{2,3,1,0:T(8,128)(2,1)}, bf16[1,8,64,32]{2,3,1,0:T(8,128)(2,1)S(1)}, u32[]{:S(2)}, u32[]{:S(2)}) collective-permute-start(bf16[1,8,64,32]{2,3,1,0:T(8,128)(2,1)} %param.3), channel_id=1, source_target_pairs={{0,8},{8,16},{16,24},{24,32},{32,40},{40,48},{48,56},{1,9},{9,17},... | collective-permute-start | bytes 98312 | tf_op jit(solution)/shard_map/ppermute | solution.py:15
  11.7 1.9 collective-permute-start.1
  13.7 4.0 %collective-permute-start.4 = (bf16[1,8,64,32]{2,3,1,0:T(8,128)(2,1)}, bf16[1,8,64,32]{2,3,1,0:T(8,128)(2,1)}, u32[]{:S(2)}, u32[]{:S(2)}) collective-permute-start(bf16[1,8,64,32]{2,3,1,0:T(8,128)(2,1)} %param.5), channel_id=1, source_target_pairs={{0,64},{64,128},{128,192},{192,256},{256,320},{320,384},{384,448},... | collective-permute-start | bytes 98312 | tf_op jit(solution)/shard_map/ppermute | solution.py:51
  17.7 8.6 %collective-permute-start.5 = (bf16[1,8,64,32]{2,3,1,0:T(8,128)(2,1)}, bf16[1,8,64,32]{2,3,1,0:T(8,128)(2,1)}, u32[]{:S(2)}, u32[]{:S(2)}) collective-permute-start(bf16[1,8,64,32]{2,3,1,0:T(8,128)(2,1)} %param.5), channel_id=1, source_target_pairs={{0,448},{64,0},{128,64},{192,128},{256,192},{320,256},{384,320},{4... | collective-permute-start | bytes 98312 | tf_op jit(solution)/shard_map/ppermute | solution.py:58
  27.2 2.1 collective-permute-start.3
  29.3 4.4 %collective-permute-start.2 = (bf16[3,1,64,32]{2,3,1,0:T(8,128)(2,1)S(1)}, bf16[3,1,64,32]{2,3,1,0:T(8,128)(2,1)S(1)}, u32[]{:S(2)}, u32[]{:S(2)}) collective-permute-start(bf16[3,1,64,32]{2,3,1,0:T(8,128)(2,1)S(1)} %get-tuple-element.62), channel_id=1, source_target_pairs={{0,1},{1,2},{2,3},{3,4},{4,5},{5,6},{6,7},{8,9},{9,10},{10,11},{11... | collective-permute-start | bytes 36872 | tf_op jit(solution)/shard_map/ppermute | solution.py:15
  34.6 1.0 copy.44
  38.5 1.0 copy.45
  39.5 1.8 dynamic_update_slice.25
  41.2 1.0 copy.46
  42.2 1.8 dynamic_update_slice.26
  44.0 1.9 collective-permute-start.6
  46.0 4.6 %collective-permute-start.7 = (bf16[1,8,64,32]{2,3,1,0:T(8,128)(2,1)}, bf16[1,8,64,32]{2,3,1,0:T(8,128)(2,1)}, u32[]{:S(2)}, u32[]{:S(2)}) collective-permute-start(bf16[1,8,64,32]{2,3,1,0:T(8,128)(2,1)} %collective-permute-done.5), channel_id=1, source_target_pairs={{0,448},{64,0},{128,64},{192,128},{256,192},{320,256},{384,320},{4... | collective-permute-start | bytes 98312 | tf_op jit(solution)/shard_map/ppermute | solution.py:58
  52.1 0.9 fusion.243
  65.7 1.9 collective-permute-start.8
  68.1 4.6 %collective-permute-start.9 = (bf16[1,8,64,32]{2,3,1,0:T(8,128)(2,1)}, bf16[1,8,64,32]{2,3,1,0:T(8,128)(2,1)S(1)}, u32[]{:S(2)}, u32[]{:S(2)}) collective-permute-start(bf16[1,8,64,32]{2,3,1,0:T(8,128)(2,1)} %collective-permute-done.7), channel_id=1, source_target_pairs={{0,448},{64,0},{128,64},{192,128},{256,192},{320,256},{384,320},{4... | collective-permute-start | bytes 98312 | tf_op jit(solution)/shard_map/ppermute | solution.py:58
  73.1 2.1 collective-permute-start.10
  76.2 1.0 copy.47
  77.2 1.8 dynamic_update_slice.27
  78.9 1.0 copy.48
  79.9 1.8 dynamic_update_slice.28
  81.9 1.8 dynamic_update_slice.29
  83.8 1.8 dynamic_update_slice.30
  86.2 2.3 collective-permute-start.12
  88.5 4.9 %collective-permute-start.11 = (bf16[1,8,64,256]{3,2,1,0:T(8,128)(2,1)S(1)}, bf16[1,8,64,256]{3,2,1,0:T(8,128)(2,1)S(1)}, u32[]{:S(2)}, u32[]{:S(2)}) collective-permute-start(bf16[1,8,64,256]{3,2,1,0:T(8,128)(2,1)S(1)} %dynamic_update_slice.31), channel_id=1, source_target_pairs={{0,8},{8,16},{16,24},{24,32},{32,40},{40,48},{48,56},{1,9},{9,17},... | collective-permute-start | bytes 786440 | tf_op jit(solution)/shard_map/ppermute | solution.py:15
  101.0 1.9 collective-permute-start.14
  102.9 4.6 %collective-permute-start.13 = (bf16[3,1,64,256]{3,2,1,0:T(8,128)(2,1)S(1)}, bf16[3,1,64,256]{3,2,1,0:T(8,128)(2,1)S(1)}, u32[]{:S(2)}, u32[]{:S(2)}) collective-permute-start(bf16[3,1,64,256]{3,2,1,0:T(8,128)(2,1)S(1)} %get-tuple-element.33), channel_id=1, source_target_pairs={{0,1},{1,2},{2,3},{3,4},{4,5},{5,6},{6,7},{8,9},{9,10},{10,11},{11... | collective-permute-start | bytes 294920 | tf_op jit(solution)/shard_map/ppermute | solution.py:15
  107.7 1.3 copy.43
  109.7 0.9 fusion.242
  116.8 178.9 %all-reduce.4.cloned.1.call-done = f32[27,32,256]{2,1,0:T(8,128)} async-done(((f32[27,32,256]{2,1,0:T(8,128)}), f32[27,32,256]{2,1,0:T(8,128)}) %all-reduce.4.cloned.1.call-update) | async-done | bytes 884752 | tf_op jit(solution)/shard_map/psum | solution.py:85
  295.7 2.2 broadcast_multiply_fusion
  297.9 1.5 convert_element_type.21
  (199 shorter events, 35.2 us)
Async XLA Ops:
  8.0 287.7 %all-reduce.4.cloned.1.call-start = ((), (), s32[]{:S(2)}) async-start(), calls=%async_computation.2 | async-start | bytes 1769472 | tf_op jit(solution)/shard_map/psum | solution.py:85
  8.0 18.2 %collective-permute-start = (bf16[1,8,64,32]{2,3,1,0:T(8,128)(2,1)}, bf16[1,8,64,32]{2,3,1,0:T(8,128)(2,1)S(1)}, u32[]{:S(2)}, u32[]{:S(2)}) collective-permute-start(bf16[1,8,64,32]{2,3,1,0:T(8,128)(2,1)} %param.3), channel_id=1, source_target_pairs={{0,8},{8,16},{16,24},{24,32},{32,40},{40,48},{48,56},{1,9},{9,17},... | collective-permute-start | bytes 98312 | tf_op jit(solution)/shard_map/ppermute | solution.py:15
  11.7 15.5 %collective-permute-start.1 = (bf16[1,8,64,32]{2,3,1,0:T(8,128)(2,1)}, bf16[1,8,64,32]{2,3,1,0:T(8,128)(2,1)S(1)}, u32[]{:S(2)}, u32[]{:S(2)}) collective-permute-start(bf16[1,8,64,32]{2,3,1,0:T(8,128)(2,1)} %param.3), channel_id=1, source_target_pairs={{8,0},{16,8},{24,16},{32,24},{40,32},{48,40},{56,48},{9,1},{17,9},... | collective-permute-start | bytes 98312 | tf_op jit(solution)/shard_map/ppermute | solution.py:16
  13.7 24.8 %collective-permute-start.4 = (bf16[1,8,64,32]{2,3,1,0:T(8,128)(2,1)}, bf16[1,8,64,32]{2,3,1,0:T(8,128)(2,1)}, u32[]{:S(2)}, u32[]{:S(2)}) collective-permute-start(bf16[1,8,64,32]{2,3,1,0:T(8,128)(2,1)} %param.5), channel_id=1, source_target_pairs={{0,64},{64,128},{128,192},{192,256},{256,320},{320,384},{384,448},... | collective-permute-start | bytes 98312 | tf_op jit(solution)/shard_map/ppermute | solution.py:51
  17.7 23.6 %collective-permute-start.5 = (bf16[1,8,64,32]{2,3,1,0:T(8,128)(2,1)}, bf16[1,8,64,32]{2,3,1,0:T(8,128)(2,1)}, u32[]{:S(2)}, u32[]{:S(2)}) collective-permute-start(bf16[1,8,64,32]{2,3,1,0:T(8,128)(2,1)} %param.5), channel_id=1, source_target_pairs={{0,448},{64,0},{128,64},{192,128},{256,192},{320,256},{384,320},{4... | collective-permute-start | bytes 98312 | tf_op jit(solution)/shard_map/ppermute | solution.py:58
  26.3 13.2 %copy-start.3 = (bf16[1,8,64,32]{2,3,1,0:T(8,128)(2,1)}, bf16[1,8,64,32]{2,3,1,0:T(8,128)(2,1)S(1)}, u32[]{:S(2)}) copy-start(bf16[1,8,64,32]{2,3,1,0:T(8,128)(2,1)S(1)} %collective-permute-done) | copy-start | bytes 98308
  27.2 23.3 %collective-permute-start.3 = (bf16[3,1,64,32]{2,3,1,0:T(8,128)(2,1)S(1)}, bf16[3,1,64,32]{2,3,1,0:T(8,128)(2,1)}, u32[]{:S(2)}, u32[]{:S(2)}) collective-permute-start(bf16[3,1,64,32]{2,3,1,0:T(8,128)(2,1)S(1)} %get-tuple-element.63), channel_id=1, source_target_pairs={{1,0},{2,1},{3,2},{4,3},{5,4},{6,5},{7,6},{9,8},{10,9},{11,10},{12... | collective-permute-start | bytes 36872 | tf_op jit(solution)/shard_map/ppermute | solution.py:16
  29.3 21.3 %collective-permute-start.2 = (bf16[3,1,64,32]{2,3,1,0:T(8,128)(2,1)S(1)}, bf16[3,1,64,32]{2,3,1,0:T(8,128)(2,1)S(1)}, u32[]{:S(2)}, u32[]{:S(2)}) collective-permute-start(bf16[3,1,64,32]{2,3,1,0:T(8,128)(2,1)S(1)} %get-tuple-element.62), channel_id=1, source_target_pairs={{0,1},{1,2},{2,3},{3,4},{4,5},{5,6},{6,7},{8,9},{9,10},{10,11},{11... | collective-permute-start | bytes 36872 | tf_op jit(solution)/shard_map/ppermute | solution.py:15
  44.0 21.6 %collective-permute-start.6 = (bf16[1,8,64,32]{2,3,1,0:T(8,128)(2,1)}, bf16[1,8,64,32]{2,3,1,0:T(8,128)(2,1)}, u32[]{:S(2)}, u32[]{:S(2)}) collective-permute-start(bf16[1,8,64,32]{2,3,1,0:T(8,128)(2,1)} %collective-permute-done.4), channel_id=1, source_target_pairs={{0,64},{64,128},{128,192},{192,256},{256,320},{320,384},{384,448},... | collective-permute-start | bytes 98312 | tf_op jit(solution)/shard_map/ppermute | solution.py:51
  46.0 22.1 %collective-permute-start.7 = (bf16[1,8,64,32]{2,3,1,0:T(8,128)(2,1)}, bf16[1,8,64,32]{2,3,1,0:T(8,128)(2,1)}, u32[]{:S(2)}, u32[]{:S(2)}) collective-permute-start(bf16[1,8,64,32]{2,3,1,0:T(8,128)(2,1)} %collective-permute-done.5), channel_id=1, source_target_pairs={{0,448},{64,0},{128,64},{192,128},{256,192},{320,256},{384,320},{4... | collective-permute-start | bytes 98312 | tf_op jit(solution)/shard_map/ppermute | solution.py:58
  50.6 0.6 copy-start.12
  52.1 2.0 copy-start
  59.6 0.8 copy-start.11
  59.9 0.8 copy-start.8
  62.2 0.8 copy-start.6
  64.7 0.8 copy-start.9
  64.9 2.7 copy-start.7
  65.7 7.4 %collective-permute-start.8 = (bf16[1,8,64,32]{2,3,1,0:T(8,128)(2,1)}, bf16[1,8,64,32]{2,3,1,0:T(8,128)(2,1)S(1)}, u32[]{:S(2)}, u32[]{:S(2)}) collective-permute-start(bf16[1,8,64,32]{2,3,1,0:T(8,128)(2,1)} %collective-permute-done.6), channel_id=1, source_target_pairs={{0,64},{64,128},{128,192},{192,256},{256,320},{320,384},{384,448},... | collective-permute-start | bytes 98312 | tf_op jit(solution)/shard_map/ppermute | solution.py:51
  68.1 15.6 %collective-permute-start.9 = (bf16[1,8,64,32]{2,3,1,0:T(8,128)(2,1)}, bf16[1,8,64,32]{2,3,1,0:T(8,128)(2,1)S(1)}, u32[]{:S(2)}, u32[]{:S(2)}) collective-permute-start(bf16[1,8,64,32]{2,3,1,0:T(8,128)(2,1)} %collective-permute-done.7), channel_id=1, source_target_pairs={{0,448},{64,0},{128,64},{192,128},{256,192},{320,256},{384,320},{4... | collective-permute-start | bytes 98312 | tf_op jit(solution)/shard_map/ppermute | solution.py:58
  73.1 12.5 %collective-permute-start.10 = (bf16[1,8,64,32]{2,3,1,0:T(8,128)(2,1)S(1)}, bf16[1,8,64,32]{2,3,1,0:T(8,128)(2,1)S(1)}, u32[]{:S(2)}, u32[]{:S(2)}) collective-permute-start(bf16[1,8,64,32]{2,3,1,0:T(8,128)(2,1)S(1)} %collective-permute-done.8), channel_id=1, source_target_pairs={{0,64},{64,128},{128,192},{192,256},{256,320},{320,384},{384,448},... | collective-permute-start | bytes 98312 | tf_op jit(solution)/shard_map/ppermute | solution.py:51
  83.8 10.5 %copy-start.4 = (bf16[1,8,64,32]{2,3,1,0:T(8,128)(2,1)S(1)}, bf16[1,8,64,32]{2,3,1,0:T(8,128)(2,1)}, u32[]{:S(2)}) copy-start(bf16[1,8,64,32]{2,3,1,0:T(8,128)(2,1)} %copy-done.3) | copy-start | bytes 98308
  86.2 14.7 %collective-permute-start.12 = (bf16[1,8,64,256]{3,2,1,0:T(8,128)(2,1)S(1)}, bf16[1,8,64,256]{3,2,1,0:T(8,128)(2,1)S(1)}, u32[]{:S(2)}, u32[]{:S(2)}) collective-permute-start(bf16[1,8,64,256]{3,2,1,0:T(8,128)(2,1)S(1)} %dynamic_update_slice.31), channel_id=1, source_target_pairs={{8,0},{16,8},{24,16},{32,24},{40,32},{48,40},{56,48},{9,1},{17,9},... | collective-permute-start | bytes 786440 | tf_op jit(solution)/shard_map/ppermute | solution.py:16
  88.5 12.4 %collective-permute-start.11 = (bf16[1,8,64,256]{3,2,1,0:T(8,128)(2,1)S(1)}, bf16[1,8,64,256]{3,2,1,0:T(8,128)(2,1)S(1)}, u32[]{:S(2)}, u32[]{:S(2)}) collective-permute-start(bf16[1,8,64,256]{3,2,1,0:T(8,128)(2,1)S(1)} %dynamic_update_slice.31), channel_id=1, source_target_pairs={{0,8},{8,16},{16,24},{24,32},{32,40},{40,48},{48,56},{1,9},{9,17},... | collective-permute-start | bytes 786440 | tf_op jit(solution)/shard_map/ppermute | solution.py:15
  95.0 1.4 copy-start.2
  98.5 2.0 copy-start.10
  99.2 1.5 copy-start.5
  99.5 0.9 copy-start.1
  100.4 197.4 %reduce-scatter.2.cloned.1.call-start = ((), (), s32[]{:S(2)}) async-start(), calls=%async_computation.1 | async-start | bytes 1179648 | tf_op jit(solution)/shard_map/reduce_scatter | solution.py:36
  101.0 8.1 %collective-permute-start.14 = (bf16[3,1,64,256]{3,2,1,0:T(8,128)(2,1)S(1)}, bf16[3,1,64,256]{3,2,1,0:T(8,128)(2,1)S(1)}, u32[]{:S(2)}, u32[]{:S(2)}) collective-permute-start(bf16[3,1,64,256]{3,2,1,0:T(8,128)(2,1)S(1)} %get-tuple-element.34), channel_id=1, source_target_pairs={{1,0},{2,1},{3,2},{4,3},{5,4},{6,5},{7,6},{9,8},{10,9},{11,10},{12... | collective-permute-start | bytes 294920 | tf_op jit(solution)/shard_map/ppermute | solution.py:16
  102.9 6.2 %collective-permute-start.13 = (bf16[3,1,64,256]{3,2,1,0:T(8,128)(2,1)S(1)}, bf16[3,1,64,256]{3,2,1,0:T(8,128)(2,1)S(1)}, u32[]{:S(2)}, u32[]{:S(2)}) collective-permute-start(bf16[3,1,64,256]{3,2,1,0:T(8,128)(2,1)S(1)} %get-tuple-element.33), channel_id=1, source_target_pairs={{0,1},{1,2},{2,3},{3,4},{4,5},{5,6},{6,7},{8,9},{9,10},{10,11},{11... | collective-permute-start | bytes 294920 | tf_op jit(solution)/shard_map/ppermute | solution.py:15
Sparse Core Ops, SparseCore 0:
  100.6 195.0 all-reduce.3
Sparse Core Ops, SparseCore 1:
  109.2 33.5 reduce-scatter.1
